TPU v7x, 32 devices: a whole 2x2x4 slice. The times are simulated.
32 devices in a mesh: panel: 2 (over y), gx: 16 (over z, x, core).
Axes of the slice: x: 2, y: 2, z: 4, core: 2. Of those that a mesh axis runs over, the one named last changes fastest.
Arguments:
- right_side: float32 [20, 1024, 256], P(None, 'gx', 'panel'), may hold values from -40 to 40
- previous: float32 [20, 1024, 256], P(None, 'gx', 'panel'), may hold values from -1.8 to 1.8
- diagonal: float32 [20, 1024, 256], P(None, 'gx', 'panel'), may hold values from 0.5 to 2
- vertical: float32 [19, 1024, 256], P(None, 'gx', 'panel'), may hold values from 0.5 to 2
- metric_a: float32 [1024, 256], P('gx', 'panel'), may hold values from 0.5 to 2
- metric_b: float32 [1024, 256], P('gx', 'panel'), may hold values from 0.5 to 2
- profile: float32 [20], replicated, may hold values from 0.5 to 2
- column_inverse: bfloat16 [4, 20, 1024, 256], P(None, None, 'gx', 'panel'), may hold values from -0.125 to 0.625, as said below
- edge_turn: int32 [4, 16, 2], replicated, may hold values from 0 to 3
Outputs:
- increment: float32 [20, 1024, 256], P(None, 'gx', 'panel')
Inputs may be any that keep to these rules, and one draw needn't show every extreme that they name: Entry column_inverse[c, k] lies in row k mod 4, column c of the inverse of the block of 4 levels that holds level k. `edge_turn`: entries 0 and 2 are read only for their lowest bit; entries 1 and 3 reverse with the lowest bit and negate with the value 2 bit.
All inputs are finite; a program needn't handle non-finite values.
Results may differ from a plain program's by a relative error of at most 0.0003.
Values sent between devices are 32-bit elements; how exact they have to be, the bound alone decides.
A program may use at most 64 MiB of HBM per device.

v0:
```python
import jax
import jax.numpy as jnp
from jax import lax
from jax.sharding import PartitionSpec as P

BK = 4


def from_behind(block, axis, distance):
    devices = range(lax.axis_size(axis))
    route = [((i - distance) % len(devices), i) for i in devices]
    return lax.ppermute(block, axis, route)


def flip_where(condition, values, dimension):
    return jnp.where(condition, jnp.flip(values, dimension), values)


def orient(values, code):
    turned = flip_where(code % 2 == 1, values, 1)
    return jnp.where(code // 2 == 1, -turned, turned)


def from_gx(values, offset):
    return from_behind(values, "gx", offset)


def from_panel(values, offset):
    return from_behind(values, "panel", offset)


def assemble(pressure, diagonal, vertical, flux_a, flux_b, high_a, high_b):
    next_a = jnp.concatenate([flux_a[:, 1:], high_a[:, None]], axis=1)
    next_b = jnp.concatenate([flux_b[:, :, 1:], high_b[:, :, None]], axis=2)
    vertical_flux = vertical * (pressure[1:] - pressure[:-1])
    zeros_row = jnp.zeros((1,) + pressure.shape[1:], jnp.float32)
    upward = jnp.concatenate([zeros_row, vertical_flux], axis=0) - jnp.concatenate(
        [vertical_flux, zeros_row], axis=0
    )
    return diagonal * pressure + (flux_a - next_a + flux_b - next_b) + upward


def local_fluxes(pressure, low_a, low_b, face_a, face_b):
    prev_a = jnp.concatenate([low_a[:, None], pressure[:, :-1]], axis=1)
    prev_b = jnp.concatenate([low_b[:, :, None], pressure[:, :, :-1]], axis=2)
    return (face_a * (pressure - prev_a), face_b * (pressure - prev_b))


def precondition(resid, column_inverse):
    level_count, rows_here, cols_here = resid.shape
    blocks = resid.reshape(level_count // BK, BK, rows_here, cols_here)
    inverse = column_inverse.reshape(BK, level_count // BK, BK, rows_here, cols_here)
    result = inverse[0].astype(jnp.float32) * blocks[:, 0:1]
    for column in range(1, BK):
        result = result + inverse[column].astype(jnp.float32) * blocks[:, column : column + 1]
    return result.reshape(level_count, rows_here, cols_here)


def shards(
    right_side, previous, diagonal, vertical, metric_a, metric_b, profile, column_inverse, edge_turn
):
    gx_index = lax.axis_index("gx")
    panel_index = lax.axis_index("panel")
    turns = edge_turn[:, gx_index, panel_index]
    face_a = metric_a[None] * profile[:, None, None]
    face_b = metric_b[None] * profile[:, None, None]

    def operate(pressure):
        low_a = flip_where(turns[0] % 2 == 1, from_gx(pressure[:, -1], 1), 1)
        low_b = flip_where(turns[2] % 2 == 1, from_panel(pressure[:, :, -1], 1), 1)
        flux_a, flux_b = local_fluxes(pressure, low_a, low_b, face_a, face_b)
        high_a = orient(from_gx(flux_a[:, 0], -1), turns[1])
        high_b = orient(from_panel(flux_b[:, :, 0], -1), turns[3])
        return assemble(pressure, diagonal, vertical, flux_a, flux_b, high_a, high_b)

    resid_first = right_side - operate(previous)
    search_first = precondition(resid_first, column_inverse)
    image_first = operate(search_first)
    cross_first, square_first = lax.psum(
        (jnp.sum(resid_first * image_first), jnp.sum(image_first * image_first)), ("panel", "gx")
    )
    alpha_first = cross_first / square_first
    resid_second = resid_first - alpha_first * image_first
    search_second = precondition(resid_second, column_inverse)
    image_second = operate(search_second)
    along_first, image_square, resid_image, resid_along = lax.psum(
        (
            jnp.sum(image_second * image_first),
            jnp.sum(image_second * image_second),
            jnp.sum(resid_second * image_second),
            jnp.sum(resid_second * image_first),
        ),
        ("panel", "gx"),
    )
    beta_coef = along_first / square_first
    alpha_second = (resid_image - beta_coef * resid_along) / (
        image_square - 2.0 * beta_coef * along_first + beta_coef * beta_coef * square_first
    )
    direction = search_second - beta_coef * search_first
    return alpha_first * search_first + alpha_second * direction


def solution(mesh):
    return jax.shard_map(
        shards,
        mesh=mesh,
        in_specs=(
            P(None, "gx", "panel"),
            P(None, "gx", "panel"),
            P(None, "gx", "panel"),
            P(None, "gx", "panel"),
            P("gx", "panel"),
            P("gx", "panel"),
            P(),
            P(None, None, "gx", "panel"),
            P(),
        ),
        out_specs=P(None, "gx", "panel"),
        check_vma=False,
    )
```

profile of v0, /device:TPU:14, one launch (start us, length us, event | category | flops | bytes accessed | tf_op | source)
XLA Modules:
  0.0 173.6 jit_solution(4378615325111884345)
XLA Ops:
  0.0 1.4 slice.165
  2.7 1.3 copy_multiply_fusion.2
  15.2 1.3 copy.378
  16.5 2.0 %multiply_multiply_fusion.5 = (f32[20,64,128]{2,0,1:T(8,128)S(1)}, f32[20,64,128]{2,0,1:T(8,128)S(1)}) fusion(f32[20,63,128]{2,0,1:T(8,128)} %slice.205, f32[20,1,128]{2,0,1:T(8,128)S(1)} %select_bitcast_fusion.5, f32[20]{0:T(128)S(1)} %copy-done.15, f32[64,128]{1,0:T(8,128)S(1)} %copy-done.13, f32[20,64,128]{2,1,0:T(8,128)S(1)} %copy-done, ...), kind=kLoop, calls=%fused_computation.5 | loop fusion | flops 1310720 | bytes 3342416 | tf_op jit(solution)/shard_map/mul | solution.py:46
  18.8 1.6 collective-permute-start.3
  22.5 1.4 collective-permute-start.1
  24.0 1.3 copy.381
  25.4 3.8 %fusion.2 = f32[20,64,128]{2,0,1:T(8,128)S(1)} fusion(f32[20,64,128]{2,1,0:T(8,128)} %param.11, f32[20,64,128]{2,0,1:T(8,128)S(1)} %get-tuple-element.27, f32[20,64,128]{2,0,1:T(8,128)S(1)} %get-tuple-element.26, f32[20,1,128]{2,0,1:T(8,128)S(1)} %fusion.19, f32[20,63,128]{2,0,1:T(8,128)} %slice.206, f32[20,64,1]{2,0,1:T(8,128)} %copy.381, ...), kind=kLoop, calls=%fused_computation.22 | loop fusion | flops 1638400 | bytes 5865472 | tf_op jit(solution)/shard_map/sub | solution.py:76
  30.7 2.1 %fusion.9 = f32[20,64,128]{2,0,1:T(8,128)S(1)} fusion(f32[20,64,128]{2,1,0:T(8,128)S(1)} %bitcast.116, f32[20,64,128]{2,1,0:T(8,128)S(1)} %bitcast.118, f32[20,64,128]{2,1,0:T(8,128)S(1)} %bitcast.119, f32[20,64,128]{2,1,0:T(8,128)S(1)} %bitcast.115, bf16[1,20,64,128]{3,2,1,0:T(8,128)(2,1)S(1)} %copy-done.10, bf16[1,20,64,128]{3,2,1,0:T(8,128)(2,1)S(1)} %copy-done.8, ...), kind=kLoop, calls=%fused_computation.29 | loop fusion | flops 1802240 | bytes 4587520 | tf_op jit(solution)/shard_map/add | solution.py:55
  32.8 1.4 copy_multiply_fusion.1
  36.3 2.3 %collective-permute-start.4 = (f32[20,128]{1,0:T(8,128)S(1)}, f32[20,128]{1,0:T(8,128)S(1)}, u32[]{:S(2)}, u32[]{:S(2)}) collective-permute-start(f32[20,128]{1,0:T(8,128)S(1)} %slice_bitcast_fusion.11), channel_id=1, source_target_pairs={{15,0},{0,1},{1,2},{2,3},{3,4},{4,5},{5,6},{6,7},{7,8},{8,9},{9,10... | collective-permute-start | bytes 30728 | tf_op jit(solution)/shard_map/ppermute | solution.py:12
  38.6 1.3 copy.397
  40.0 1.7 multiply_multiply_fusion.4
  42.6 1.5 collective-permute-start.7
  49.6 3.9 %multiply_reduce_fusion.4 = (f32[]{:T(128)}, f32[]{:T(128)}, f32[20,64,128]{2,0,1:T(8,128)S(1)}) fusion(f32[20,64,128]{2,0,1:T(8,128)S(1)} %fusion.2, f32[19,64,128]{2,0,1:T(8,128)} %copy_multiply_fusion.1, f32[20,64,1]{2,0,1:T(8,128)} %copy.399, f32[20,64,127]{2,0,1:T(8,128)} %slice.223, f32[20,64,128]{2,0,1:T(8,128)S(1)} %get-tuple-element.25, ...), kind=kLoop, calls=%fused_computation.57 | loop fusion | flops 2129918 | bytes 5865480 | tf_op jit(solution)/shard_map/reduce_sum | solution.py:80
  53.6 44.5 %all-reduce.7 = (f32[]{:T(128)}, f32[]{:T(128)}) all-reduce(f32[]{:T(128)} %get-tuple-element.10, f32[]{:T(128)} %get-tuple-element.9), channel_id=1, replica_groups=mesh['panel'=2,'gx'=16] {'panel','gx'}, use_global_device_ids=true, to_apply=%region_1.2 | all-reduce | flops 2 | bytes 16 | tf_op jit(solution)/shard_map/psum | solution.py:79
  101.6 2.1 %fusion.12 = f32[20,64,128]{2,0,1:T(8,128)S(1)} fusion(f32[20,64,128]{2,1,0:T(8,128)S(1)} %bitcast.113, f32[20,64,128]{2,1,0:T(8,128)S(1)} %bitcast.114, f32[20,64,128]{2,1,0:T(8,128)S(1)} %bitcast.117, f32[20,64,128]{2,1,0:T(8,128)S(1)} %bitcast.112, bf16[1,20,64,128]{3,2,1,0:T(8,128)(2,1)S(1)} %copy-done.11, bf16[1,20,64,128]{3,2,1,0:T(8,128)(2,1)S(1)} %copy-done.9, ...), kind=kLoop, calls=%fused_computation.32 | loop fusion | flops 1802240 | bytes 4587520 | tf_op jit(solution)/shard_map/add | solution.py:55
  103.8 1.4 copy_multiply_fusion
  107.8 1.7 collective-permute-done.10
  111.0 2.6 %multiply_multiply_fusion.3 = (f32[20,64,128]{2,0,1:T(8,128)}, f32[20,64,128]{2,0,1:T(8,128)S(1)}) fusion(f32[20,64,128]{2,0,1:T(8,128)S(1)} %fusion.12, f32[20,63,128]{2,0,1:T(8,128)} %slice.232, f32[20,1,128]{2,0,1:T(8,128)S(1)} %select_bitcast_fusion.1, f32[20]{0:T(128)S(1)} %copy-done.15, f32[64,128]{1,0:T(8,128)S(1)} %copy-done.13, ...), kind=kLoop, calls=%fused_computation.3 | loop fusion | flops 1310720 | bytes 3342416 | tf_op jit(solution)/shard_map/mul | solution.py:46
  115.6 2.1 %slice.233 = f32[20,63,128]{2,0,1:T(8,128)} slice(f32[20,64,128]{2,0,1:T(8,128)} %get-tuple-element.22), slice={[0:20], [1:64], [0:128]} | slice | bytes 1290240 | tf_op jit(solution)/shard_map/slice | solution.py:33
  119.0 1.2 copy.410
  120.4 4.3 %multiply_reduce_fusion = (f32[]{:T(128)}, f32[]{:T(128)}, f32[]{:T(128)}, f32[]{:T(128)}) fusion(f32[20,64,128]{2,0,1:T(8,128)S(1)} %get-tuple-element.17, f32[20,64,128]{2,0,1:T(8,128)} %copy-done.2, f32[19,64,128]{2,0,1:T(8,128)} %copy_multiply_fusion, f32[20,64,1]{2,0,1:T(8,128)} %copy.410, f32[20,64,127]{2,0,1:T(8,128)} %slice.237, ...), kind=kLoop, calls=%fused_computation.52 | loop fusion | flops 2785276 | bytes 5865488 | tf_op jit(solution)/shard_map/reduce_sum | solution.py:89
  124.6 43.4 %all-reduce.6 = (f32[]{:T(128)}, f32[]{:T(128)}, f32[]{:T(128)}, f32[]{:T(128)}) all-reduce(f32[]{:T(128)} %get-tuple-element.6, f32[]{:T(128)} %get-tuple-element.8, f32[]{:T(128)} %get-tuple-element.7, f32[]{:T(128)} %get-tuple-element.5), channel_id=1, replica_groups=mesh['panel'=2,'gx'=16] {'panel','gx'}, use_global_device_ids=true, to_apply=%region_7.8 | all-reduce | flops 4 | bytes 32 | tf_op jit(solution)/shard_map/psum | solution.py:86
  (119 shorter events, 27.6 us)
Async XLA Ops:
  0.0 2.2 %copy-start = (f32[20,64,128]{2,1,0:T(8,128)S(1)}, f32[20,64,128]{2,1,0:T(8,128)}, u32[]{:S(2)}) copy-start(f32[20,64,128]{2,1,0:T(8,128)} %param.10) | copy-start | bytes 1966084
  1.4 1.3 copy-start.3
  1.7 13.4 %collective-permute-start.2 = (f32[20,64]{1,0:T(8,128)S(1)}, f32[20,64]{1,0:T(8,128)S(1)}, u32[]{:S(2)}, u32[]{:S(2)}) collective-permute-start(f32[20,64]{1,0:T(8,128)S(1)} %bitcast.126), channel_id=1, source_target_pairs={{16,0},{0,16},{17,1},{1,17},{18,2},{2,18},{19,3},{3,19},{20,4},{4,... | collective-permute-start | bytes 15368 | tf_op jit(solution)/shard_map/ppermute | solution.py:12
  2.6 13.8 %collective-permute-start = (f32[20,128]{1,0:T(8,128)S(1)}, f32[20,128]{1,0:T(8,128)S(1)}, u32[]{:S(2)}, u32[]{:S(2)}) collective-permute-start(f32[20,128]{1,0:T(8,128)S(1)} %slice_bitcast_fusion.13), channel_id=1, source_target_pairs={{15,0},{0,1},{1,2},{2,3},{3,4},{4,5},{5,6},{6,7},{7,8},{8,9},{9,10... | collective-permute-start | bytes 30728 | tf_op jit(solution)/shard_map/ppermute | solution.py:12
  2.7 1.3 copy-start.12
  5.7 10.8 %copy-start.13 = (f32[64,128]{1,0:T(8,128)S(1)}, f32[64,128]{1,0:T(8,128)}, u32[]{:S(2)}) copy-start(f32[64,128]{1,0:T(8,128)} %param.13) | copy-start | bytes 98308
  5.7 10.8 %copy-start.14 = (f32[64,128]{1,0:T(8,128)S(1)}, f32[64,128]{1,0:T(8,128)}, u32[]{:S(2)}) copy-start(f32[64,128]{1,0:T(8,128)} %param.14) | copy-start | bytes 98308
  5.7 10.8 %copy-start.15 = (f32[20]{0:T(128)S(1)}, f32[20]{0:T(128)}, u32[]{:S(2)}) copy-start(f32[20]{0:T(128)} %param.15) | copy-start | bytes 244
  18.8 5.1 %collective-permute-start.3 = (f32[20,64]{1,0:T(8,128)S(1)}, f32[20,64]{1,0:T(8,128)S(1)}, u32[]{:S(2)}, u32[]{:S(2)}) collective-permute-start(f32[20,64]{1,0:T(8,128)S(1)} %bitcast.122), channel_id=1, source_target_pairs={{16,0},{0,16},{17,1},{1,17},{18,2},{2,18},{19,3},{3,19},{20,4},{4,... | collective-permute-start | bytes 15368 | tf_op jit(solution)/shard_map/ppermute | solution.py:12
  22.5 2.8 %collective-permute-start.1 = (f32[20,128]{1,0:T(8,128)S(1)}, f32[20,128]{1,0:T(8,128)S(1)}, u32[]{:S(2)}, u32[]{:S(2)}) collective-permute-start(f32[20,128]{1,0:T(8,128)S(1)} %slice_bitcast_fusion.12), channel_id=1, source_target_pairs={{1,0},{2,1},{3,2},{4,3},{5,4},{6,5},{7,6},{8,7},{9,8},{10,9},{11,1... | collective-permute-start | bytes 30728 | tf_op jit(solution)/shard_map/ppermute | solution.py:12
  29.5 1.1 copy-start.8
  29.5 1.2 copy-start.10
  30.7 2.1 %copy-start.4 = (f32[19,64,128]{2,1,0:T(8,128)S(1)}, f32[19,64,128]{2,1,0:T(8,128)}, u32[]{:S(2)}) copy-start(f32[19,64,128]{2,1,0:T(8,128)} %param.12) | copy-start | bytes 1867780
  34.8 3.8 %collective-permute-start.6 = (f32[20,64]{1,0:T(8,128)S(1)}, f32[20,64]{1,0:T(8,128)S(1)}, u32[]{:S(2)}, u32[]{:S(2)}) collective-permute-start(f32[20,64]{1,0:T(8,128)S(1)} %bitcast.124), channel_id=1, source_target_pairs={{16,0},{0,16},{17,1},{1,17},{18,2},{2,18},{19,3},{3,19},{20,4},{4,... | collective-permute-start | bytes 15368 | tf_op jit(solution)/shard_map/ppermute | solution.py:12
  36.3 3.6 %collective-permute-start.4 = (f32[20,128]{1,0:T(8,128)S(1)}, f32[20,128]{1,0:T(8,128)S(1)}, u32[]{:S(2)}, u32[]{:S(2)}) collective-permute-start(f32[20,128]{1,0:T(8,128)S(1)} %slice_bitcast_fusion.11), channel_id=1, source_target_pairs={{15,0},{0,1},{1,2},{2,3},{3,4},{4,5},{5,6},{6,7},{7,8},{8,9},{9,10... | collective-permute-start | bytes 30728 | tf_op jit(solution)/shard_map/ppermute | solution.py:12
  41.7 5.2 %copy-start.1 = (f32[20,64,128]{2,0,1:T(8,128)}, f32[20,64,128]{2,0,1:T(8,128)S(1)}, u32[]{:S(2)}) copy-start(f32[20,64,128]{2,0,1:T(8,128)S(1)} %get-tuple-element.24) | copy-start | bytes 1966084
  42.6 4.2 %collective-permute-start.7 = (f32[20,64]{1,0:T(8,128)}, f32[20,64]{1,0:T(8,128)}, u32[]{:S(2)}, u32[]{:S(2)}) collective-permute-start(f32[20,64]{1,0:T(8,128)} %bitcast.31), channel_id=1, source_target_pairs={{16,0},{0,16},{17,1},{1,17},{18,2},{2,18},{19,3},{3,19},{20,4},{4,... | collective-permute-start | bytes 15368 | tf_op jit(solution)/shard_map/ppermute | solution.py:12
  46.8 2.7 %collective-permute-start.5 = (f32[20,128]{1,0:T(8,128)}, f32[20,128]{1,0:T(8,128)S(1)}, u32[]{:S(2)}, u32[]{:S(2)}) collective-permute-start(f32[20,128]{1,0:T(8,128)} %slice_bitcast_fusion.10), channel_id=1, source_target_pairs={{1,0},{2,1},{3,2},{4,3},{5,4},{6,5},{7,6},{8,7},{9,8},{10,9},{11,1... | collective-permute-start | bytes 30728 | tf_op jit(solution)/shard_map/ppermute | solution.py:12
  100.5 1.2 copy-start.11
  101.6 2.1 %copy-start.5 = (f32[19,64,128]{2,1,0:T(8,128)S(1)}, f32[19,64,128]{2,1,0:T(8,128)}, u32[]{:S(2)}) copy-start(f32[19,64,128]{2,1,0:T(8,128)} %param.12) | copy-start | bytes 1867780
  105.8 3.7 %collective-permute-start.10 = (f32[20,64]{1,0:T(8,128)S(1)}, f32[20,64]{1,0:T(8,128)S(1)}, u32[]{:S(2)}, u32[]{:S(2)}) collective-permute-start(f32[20,64]{1,0:T(8,128)S(1)} %bitcast.125), channel_id=1, source_target_pairs={{16,0},{0,16},{17,1},{1,17},{18,2},{2,18},{19,3},{3,19},{20,4},{4,... | collective-permute-start | bytes 15368 | tf_op jit(solution)/shard_map/ppermute | solution.py:12
  107.8 3.1 %collective-permute-start.8 = (f32[20,128]{1,0:T(8,128)S(1)}, f32[20,128]{1,0:T(8,128)S(1)}, u32[]{:S(2)}, u32[]{:S(2)}) collective-permute-start(f32[20,128]{1,0:T(8,128)S(1)} %slice_bitcast_fusion.9), channel_id=1, source_target_pairs={{15,0},{0,1},{1,2},{2,3},{3,4},{4,5},{5,6},{6,7},{7,8},{8,9},{9,10... | collective-permute-start | bytes 30728 | tf_op jit(solution)/shard_map/ppermute | solution.py:12
  113.9 4.9 %collective-permute-start.11 = (f32[20,64]{1,0:T(8,128)S(1)}, f32[20,64]{1,0:T(8,128)S(1)}, u32[]{:S(2)}, u32[]{:S(2)}) collective-permute-start(f32[20,64]{1,0:T(8,128)S(1)} %bitcast.123), channel_id=1, source_target_pairs={{16,0},{0,16},{17,1},{1,17},{18,2},{2,18},{19,3},{3,19},{20,4},{4,... | collective-permute-start | bytes 15368 | tf_op jit(solution)/shard_map/ppermute | solution.py:12
  118.9 1.4 collective-permute-start.9
  (5 other events, 4.9 us)
where the time goes:
time: 175 us; the launch traced here: 174 us
  blocking collectives  87.9 us (50%)
  local copies, waits for them, and re-layouts  31.4 us (18%)
  other arithmetic  27.7 us (16%)
  between operations  14.6 us (8%)
  starting transfers between devices  10 us (6%)
  waiting for transfers between devices  1.99 us (1%)
    psum x1, blocking collectives, shards(): lax.psum((jnp.sum(resid_first * image_first), jnp.sum(image_first * image...  44.5 us
    psum x1, blocking collectives, shards(): lax.psum((jnp.sum(image_second * image_first), jnp.sum(image_second * ima...  43.4 us
    ppermute x12, starting transfers between devices, from_behind(): return lax.ppermute(block, axis, route)  10 us
    mul x3, other arithmetic, local_fluxes(): return (face_a * (pressure - prev_a), face_b * (pressure - prev_b))  6.31 us
    reduce_sum x1, other arithmetic, shards(): jnp.sum(image_second * image_second)  4.28 us
    add x2, other arithmetic, precondition(): result + inverse[column].astype(jnp.float32) * blocks[:, column:column + 1]  4.25 us
    mul x3, other arithmetic, assemble(): vertical_flux = vertical * (pressure[1:] - pressure[:-1])  4.12 us
    slice x3, local copies, waits for them, and re-layouts, assemble(): next_a = jnp.concatenate([flux_a[:, 1:], high_a[:, None]], axis=1)  3.94 us
  transfers between devices with their start and end apart: 12, of which 4 were waited for; matrix products, arithmetic and copies ran while one was open for 14% of the time, Pallas kernels for 0%

commit v1 on v0

--- a/solution.py
+++ b/solution.py
@@ -77,7 +77,8 @@
     search_first = precondition(resid_first, column_inverse)
     image_first = operate(search_first)
     cross_first, square_first = lax.psum(
-        (jnp.sum(resid_first * image_first), jnp.sum(image_first * image_first)), ("panel", "gx")
+        lax.psum((jnp.sum(resid_first * image_first), jnp.sum(image_first * image_first)), "gx"),
+        "panel",
     )
     alpha_first = cross_first / square_first
     resid_second = resid_first - alpha_first * image_first

time: 175 us -> 175 us (level)
  blocking collectives: 87.9 us -> 85.1 us
  starting transfers between devices: 10 us -> 12.4 us
    psum x1, blocking collectives: 44.5 us -> 26 us  [shards(): lax.psum((jnp.sum(resid_first * image_first), jnp.sum(image_first * image...]
    psum x1, blocking collectives: 43.4 us -> 53.3 us  [shards(): lax.psum((jnp.sum(image_second * image_first), jnp.sum(image_second * ima...]
    psum x0 -> x1, blocking collectives: none -> 5.8 us  [shards(): lax.psum(lax.psum((jnp.sum(resid_first * image_first), jnp.sum(image_firs...]
    ppermute x12, starting transfers between devices: 10 us -> 12.4 us  [from_behind(): return lax.ppermute(block, axis, route)]
where the time goes in v1:
time: 175 us; the launch traced here: 174 us
  blocking collectives  85.1 us (49%)
  local copies, waits for them, and re-layouts  31.4 us (18%)
  other arithmetic  27.7 us (16%)
  between operations  15.2 us (9%)
  starting transfers between devices  12.4 us (7%)
  waiting for transfers between devices  1.99 us (1%)
    psum x1, blocking collectives, shards(): lax.psum((jnp.sum(image_second * image_first), jnp.sum(image_second * ima...  53.3 us
    psum x1, blocking collectives, shards(): lax.psum((jnp.sum(resid_first * image_first), jnp.sum(image_first * image...  26 us
    ppermute x12, starting transfers between devices, from_behind(): return lax.ppermute(block, axis, route)  12.4 us
    mul x3, other arithmetic, local_fluxes(): return (face_a * (pressure - prev_a), face_b * (pressure - prev_b))  6.29 us
    psum x1, blocking collectives, shards(): lax.psum(lax.psum((jnp.sum(resid_first * image_first), jnp.sum(image_firs...  5.8 us
    reduce_sum x1, other arithmetic, shards(): jnp.sum(image_second * image_second)  4.25 us
    add x2, other arithmetic, precondition(): result + inverse[column].astype(jnp.float32) * blocks[:, column:column + 1]  4.25 us
    mul x3, other arithmetic, assemble(): vertical_flux = vertical * (pressure[1:] - pressure[:-1])  4.15 us
  transfers between devices with their start and end apart: 12, of which 4 were waited for; matrix products, arithmetic and copies ran while one was open for 14% of the time, Pallas kernels for 0%

profile of v1, /device:TPU:14, one launch (start us, length us, event | category | flops | bytes accessed | tf_op | source)
XLA Modules:
  0.0 173.7 jit_solution(14851721645743250254)
XLA Ops:
  0.0 1.4 slice.165
  2.7 1.3 copy_multiply_fusion.2
  15.8 1.3 copy.378
  17.1 2.0 %multiply_multiply_fusion.5 = (f32[20,64,128]{2,0,1:T(8,128)S(1)}, f32[20,64,128]{2,0,1:T(8,128)S(1)}) fusion(f32[20,63,128]{2,0,1:T(8,128)} %slice.205, f32[20,1,128]{2,0,1:T(8,128)S(1)} %select_bitcast_fusion.5, f32[20]{0:T(128)S(1)} %copy-done.15, f32[64,128]{1,0:T(8,128)S(1)} %copy-done.13, f32[20,64,128]{2,1,0:T(8,128)S(1)} %copy-done, ...), kind=kLoop, calls=%fused_computation.5 | loop fusion | flops 1310720 | bytes 3342416 | tf_op jit(solution)/shard_map/mul | solution.py:46
  19.4 1.6 collective-permute-start.3
  23.1 1.4 collective-permute-start.1
  26.0 3.8 %fusion.2 = f32[20,64,128]{2,0,1:T(8,128)S(1)} fusion(f32[20,64,128]{2,1,0:T(8,128)} %param.11, f32[20,64,128]{2,0,1:T(8,128)S(1)} %get-tuple-element.29, f32[20,64,128]{2,0,1:T(8,128)S(1)} %get-tuple-element.28, f32[20,1,128]{2,0,1:T(8,128)S(1)} %fusion.19, f32[20,63,128]{2,0,1:T(8,128)} %slice.206, f32[20,64,1]{2,0,1:T(8,128)} %copy.381, ...), kind=kLoop, calls=%fused_computation.22 | loop fusion | flops 1638400 | bytes 5865472 | tf_op jit(solution)/shard_map/sub | solution.py:76
  31.3 2.1 %fusion.9 = f32[20,64,128]{2,0,1:T(8,128)S(1)} fusion(f32[20,64,128]{2,1,0:T(8,128)S(1)} %bitcast.116, f32[20,64,128]{2,1,0:T(8,128)S(1)} %bitcast.118, f32[20,64,128]{2,1,0:T(8,128)S(1)} %bitcast.119, f32[20,64,128]{2,1,0:T(8,128)S(1)} %bitcast.115, bf16[1,20,64,128]{3,2,1,0:T(8,128)(2,1)S(1)} %copy-done.10, bf16[1,20,64,128]{3,2,1,0:T(8,128)(2,1)S(1)} %copy-done.8, ...), kind=kLoop, calls=%fused_computation.29 | loop fusion | flops 1802240 | bytes 4587520 | tf_op jit(solution)/shard_map/add | solution.py:55
  33.4 1.4 copy_multiply_fusion.1
  36.9 2.3 %collective-permute-start.4 = (f32[20,128]{1,0:T(8,128)S(1)}, f32[20,128]{1,0:T(8,128)S(1)}, u32[]{:S(2)}, u32[]{:S(2)}) collective-permute-start(f32[20,128]{1,0:T(8,128)S(1)} %slice_bitcast_fusion.11), channel_id=1, source_target_pairs={{15,0},{0,1},{1,2},{2,3},{3,4},{4,5},{5,6},{6,7},{7,8},{8,9},{9,10... | collective-permute-start | bytes 30728 | tf_op jit(solution)/shard_map/ppermute | solution.py:12
  40.5 1.7 multiply_multiply_fusion.4
  43.2 1.5 collective-permute-start.7
  50.2 3.9 %multiply_reduce_fusion.4 = (f32[]{:T(128)}, f32[]{:T(128)}, f32[20,64,128]{2,0,1:T(8,128)S(1)}) fusion(f32[20,64,128]{2,0,1:T(8,128)S(1)} %fusion.2, f32[19,64,128]{2,0,1:T(8,128)} %copy_multiply_fusion.1, f32[20,64,1]{2,0,1:T(8,128)} %copy.399, f32[20,64,127]{2,0,1:T(8,128)} %slice.223, f32[20,64,128]{2,0,1:T(8,128)S(1)} %get-tuple-element.27, ...), kind=kLoop, calls=%fused_computation.57 | loop fusion | flops 2129918 | bytes 5865480 | tf_op jit(solution)/shard_map/reduce_sum | solution.py:80
  54.1 26.0 %all-reduce.7 = (f32[]{:T(128)}, f32[]{:T(128)}) all-reduce(f32[]{:T(128)} %get-tuple-element.10, f32[]{:T(128)} %get-tuple-element.9), channel_id=1, replica_groups=mesh['panel'=2,'gx'=16] {'gx'}, use_global_device_ids=true, to_apply=%region_1.2 | all-reduce | flops 2 | bytes 16 | tf_op jit(solution)/shard_map/psum | solution.py:80
  80.1 5.8 %all-reduce.8 = (f32[]{:T(128)}, f32[]{:T(128)}) all-reduce(f32[]{:T(128)} %get-tuple-element.15, f32[]{:T(128)} %get-tuple-element.16), channel_id=1, replica_groups=mesh['panel'=2,'gx'=16] {'panel'}, use_global_device_ids=true, to_apply=%region_2.3 | all-reduce | flops 2 | bytes 16 | tf_op jit(solution)/shard_map/psum | solution.py:79
  89.4 2.1 %fusion.12 = f32[20,64,128]{2,0,1:T(8,128)S(1)} fusion(f32[20,64,128]{2,1,0:T(8,128)S(1)} %bitcast.113, f32[20,64,128]{2,1,0:T(8,128)S(1)} %bitcast.114, f32[20,64,128]{2,1,0:T(8,128)S(1)} %bitcast.117, f32[20,64,128]{2,1,0:T(8,128)S(1)} %bitcast.112, bf16[1,20,64,128]{3,2,1,0:T(8,128)(2,1)S(1)} %copy-done.11, bf16[1,20,64,128]{3,2,1,0:T(8,128)(2,1)S(1)} %copy-done.9, ...), kind=kLoop, calls=%fused_computation.32 | loop fusion | flops 1802240 | bytes 4587520 | tf_op jit(solution)/shard_map/add | solution.py:55
  91.6 1.4 copy_multiply_fusion
  93.6 1.3 collective-permute-start.10
  95.8 1.5 collective-permute-done.10
  99.0 2.6 %multiply_multiply_fusion.3 = (f32[20,64,128]{2,0,1:T(8,128)}, f32[20,64,128]{2,0,1:T(8,128)S(1)}) fusion(f32[20,64,128]{2,0,1:T(8,128)S(1)} %fusion.12, f32[20,63,128]{2,0,1:T(8,128)} %slice.232, f32[20,1,128]{2,0,1:T(8,128)S(1)} %select_bitcast_fusion.1, f32[20]{0:T(128)S(1)} %copy-done.15, f32[64,128]{1,0:T(8,128)S(1)} %copy-done.13, ...), kind=kLoop, calls=%fused_computation.3 | loop fusion | flops 1310720 | bytes 3342416 | tf_op jit(solution)/shard_map/mul | solution.py:46
  103.6 2.1 %slice.233 = f32[20,63,128]{2,0,1:T(8,128)} slice(f32[20,64,128]{2,0,1:T(8,128)} %get-tuple-element.24), slice={[0:20], [1:64], [0:128]} | slice | bytes 1290240 | tf_op jit(solution)/shard_map/slice | solution.py:33
  106.8 2.2 %collective-permute-start.9 = (f32[20,128]{1,0:T(8,128)S(1)}, f32[20,128]{1,0:T(8,128)S(1)}, u32[]{:S(2)}, u32[]{:S(2)}) collective-permute-start(f32[20,128]{1,0:T(8,128)S(1)} %slice_bitcast_fusion.8), channel_id=1, source_target_pairs={{1,0},{2,1},{3,2},{4,3},{5,4},{6,5},{7,6},{8,7},{9,8},{10,9},{11,1... | collective-permute-start | bytes 30728 | tf_op jit(solution)/shard_map/ppermute | solution.py:12
  110.5 4.3 %multiply_reduce_fusion = (f32[]{:T(128)}, f32[]{:T(128)}, f32[]{:T(128)}, f32[]{:T(128)}) fusion(f32[20,64,128]{2,0,1:T(8,128)S(1)} %get-tuple-element.19, f32[20,64,128]{2,0,1:T(8,128)} %copy-done.2, f32[19,64,128]{2,0,1:T(8,128)} %copy_multiply_fusion, f32[20,64,1]{2,0,1:T(8,128)} %copy.410, f32[20,64,127]{2,0,1:T(8,128)} %slice.237, ...), kind=kLoop, calls=%fused_computation.52 | loop fusion | flops 2785276 | bytes 5865488 | tf_op jit(solution)/shard_map/reduce_sum | solution.py:90
  114.7 53.3 %all-reduce.6 = (f32[]{:T(128)}, f32[]{:T(128)}, f32[]{:T(128)}, f32[]{:T(128)}) all-reduce(f32[]{:T(128)} %get-tuple-element.6, f32[]{:T(128)} %get-tuple-element.8, f32[]{:T(128)} %get-tuple-element.7, f32[]{:T(128)} %get-tuple-element.5), channel_id=1, replica_groups=mesh['panel'=2,'gx'=16] {'panel','gx'}, use_global_device_ids=true, to_apply=%region_9.10 | all-reduce | flops 4 | bytes 32 | tf_op jit(solution)/shard_map/psum | solution.py:87
  (120 shorter events, 30.3 us)
Async XLA Ops:
  0.0 2.2 %copy-start = (f32[20,64,128]{2,1,0:T(8,128)S(1)}, f32[20,64,128]{2,1,0:T(8,128)}, u32[]{:S(2)}) copy-start(f32[20,64,128]{2,1,0:T(8,128)} %param.10) | copy-start | bytes 1966084
  1.4 1.3 copy-start.3
  1.7 14.0 %collective-permute-start.2 = (f32[20,64]{1,0:T(8,128)S(1)}, f32[20,64]{1,0:T(8,128)S(1)}, u32[]{:S(2)}, u32[]{:S(2)}) collective-permute-start(f32[20,64]{1,0:T(8,128)S(1)} %bitcast.126), channel_id=1, source_target_pairs={{16,0},{0,16},{17,1},{1,17},{18,2},{2,18},{19,3},{3,19},{20,4},{4,... | collective-permute-start | bytes 15368 | tf_op jit(solution)/shard_map/ppermute | solution.py:12
  2.6 14.4 %collective-permute-start = (f32[20,128]{1,0:T(8,128)S(1)}, f32[20,128]{1,0:T(8,128)S(1)}, u32[]{:S(2)}, u32[]{:S(2)}) collective-permute-start(f32[20,128]{1,0:T(8,128)S(1)} %slice_bitcast_fusion.13), channel_id=1, source_target_pairs={{15,0},{0,1},{1,2},{2,3},{3,4},{4,5},{5,6},{6,7},{7,8},{8,9},{9,10... | collective-permute-start | bytes 30728 | tf_op jit(solution)/shard_map/ppermute | solution.py:12
  2.7 1.3 copy-start.12
  5.7 11.4 %copy-start.13 = (f32[64,128]{1,0:T(8,128)S(1)}, f32[64,128]{1,0:T(8,128)}, u32[]{:S(2)}) copy-start(f32[64,128]{1,0:T(8,128)} %param.13) | copy-start | bytes 98308
  5.7 11.4 %copy-start.14 = (f32[64,128]{1,0:T(8,128)S(1)}, f32[64,128]{1,0:T(8,128)}, u32[]{:S(2)}) copy-start(f32[64,128]{1,0:T(8,128)} %param.14) | copy-start | bytes 98308
  5.7 11.4 %copy-start.15 = (f32[20]{0:T(128)S(1)}, f32[20]{0:T(128)}, u32[]{:S(2)}) copy-start(f32[20]{0:T(128)} %param.15) | copy-start | bytes 244
  19.4 5.1 %collective-permute-start.3 = (f32[20,64]{1,0:T(8,128)S(1)}, f32[20,64]{1,0:T(8,128)S(1)}, u32[]{:S(2)}, u32[]{:S(2)}) collective-permute-start(f32[20,64]{1,0:T(8,128)S(1)} %bitcast.122), channel_id=1, source_target_pairs={{16,0},{0,16},{17,1},{1,17},{18,2},{2,18},{19,3},{3,19},{20,4},{4,... | collective-permute-start | bytes 15368 | tf_op jit(solution)/shard_map/ppermute | solution.py:12
  23.1 2.8 %collective-permute-start.1 = (f32[20,128]{1,0:T(8,128)S(1)}, f32[20,128]{1,0:T(8,128)S(1)}, u32[]{:S(2)}, u32[]{:S(2)}) collective-permute-start(f32[20,128]{1,0:T(8,128)S(1)} %slice_bitcast_fusion.12), channel_id=1, source_target_pairs={{1,0},{2,1},{3,2},{4,3},{5,4},{6,5},{7,6},{8,7},{9,8},{10,9},{11,1... | collective-permute-start | bytes 30728 | tf_op jit(solution)/shard_map/ppermute | solution.py:12
  30.1 1.1 copy-start.8
  30.1 1.2 copy-start.10
  31.3 2.1 %copy-start.4 = (f32[19,64,128]{2,1,0:T(8,128)S(1)}, f32[19,64,128]{2,1,0:T(8,128)}, u32[]{:S(2)}) copy-start(f32[19,64,128]{2,1,0:T(8,128)} %param.12) | copy-start | bytes 1867780
  35.4 3.7 %collective-permute-start.6 = (f32[20,64]{1,0:T(8,128)S(1)}, f32[20,64]{1,0:T(8,128)S(1)}, u32[]{:S(2)}, u32[]{:S(2)}) collective-permute-start(f32[20,64]{1,0:T(8,128)S(1)} %bitcast.124), channel_id=1, source_target_pairs={{16,0},{0,16},{17,1},{1,17},{18,2},{2,18},{19,3},{3,19},{20,4},{4,... | collective-permute-start | bytes 15368 | tf_op jit(solution)/shard_map/ppermute | solution.py:12
  36.9 3.6 %collective-permute-start.4 = (f32[20,128]{1,0:T(8,128)S(1)}, f32[20,128]{1,0:T(8,128)S(1)}, u32[]{:S(2)}, u32[]{:S(2)}) collective-permute-start(f32[20,128]{1,0:T(8,128)S(1)} %slice_bitcast_fusion.11), channel_id=1, source_target_pairs={{15,0},{0,1},{1,2},{2,3},{3,4},{4,5},{5,6},{6,7},{7,8},{8,9},{9,10... | collective-permute-start | bytes 30728 | tf_op jit(solution)/shard_map/ppermute | solution.py:12
  42.3 5.1 %copy-start.1 = (f32[20,64,128]{2,0,1:T(8,128)}, f32[20,64,128]{2,0,1:T(8,128)S(1)}, u32[]{:S(2)}) copy-start(f32[20,64,128]{2,0,1:T(8,128)S(1)} %get-tuple-element.26) | copy-start | bytes 1966084
  43.2 4.2 %collective-permute-start.7 = (f32[20,64]{1,0:T(8,128)}, f32[20,64]{1,0:T(8,128)}, u32[]{:S(2)}, u32[]{:S(2)}) collective-permute-start(f32[20,64]{1,0:T(8,128)} %bitcast.31), channel_id=1, source_target_pairs={{16,0},{0,16},{17,1},{1,17},{18,2},{2,18},{19,3},{3,19},{20,4},{4,... | collective-permute-start | bytes 15368 | tf_op jit(solution)/shard_map/ppermute | solution.py:12
  47.4 2.7 %collective-permute-start.5 = (f32[20,128]{1,0:T(8,128)}, f32[20,128]{1,0:T(8,128)S(1)}, u32[]{:S(2)}, u32[]{:S(2)}) collective-permute-start(f32[20,128]{1,0:T(8,128)} %slice_bitcast_fusion.10), channel_id=1, source_target_pairs={{1,0},{2,1},{3,2},{4,3},{5,4},{6,5},{7,6},{8,7},{9,8},{10,9},{11,1... | collective-permute-start | bytes 30728 | tf_op jit(solution)/shard_map/ppermute | solution.py:12
  88.3 1.2 copy-start.11
  89.4 2.1 %copy-start.5 = (f32[19,64,128]{2,1,0:T(8,128)S(1)}, f32[19,64,128]{2,1,0:T(8,128)}, u32[]{:S(2)}) copy-start(f32[19,64,128]{2,1,0:T(8,128)} %param.12) | copy-start | bytes 1867780
  93.6 3.7 %collective-permute-start.10 = (f32[20,64]{1,0:T(8,128)S(1)}, f32[20,64]{1,0:T(8,128)S(1)}, u32[]{:S(2)}, u32[]{:S(2)}) collective-permute-start(f32[20,64]{1,0:T(8,128)S(1)} %bitcast.125), channel_id=1, source_target_pairs={{16,0},{0,16},{17,1},{1,17},{18,2},{2,18},{19,3},{3,19},{20,4},{4,... | collective-permute-start | bytes 15368 | tf_op jit(solution)/shard_map/ppermute | solution.py:12
  95.8 3.1 %collective-permute-start.8 = (f32[20,128]{1,0:T(8,128)S(1)}, f32[20,128]{1,0:T(8,128)S(1)}, u32[]{:S(2)}, u32[]{:S(2)}) collective-permute-start(f32[20,128]{1,0:T(8,128)S(1)} %slice_bitcast_fusion.9), channel_id=1, source_target_pairs={{15,0},{0,1},{1,2},{2,3},{3,4},{4,5},{5,6},{6,7},{7,8},{8,9},{9,10... | collective-permute-start | bytes 30728 | tf_op jit(solution)/shard_map/ppermute | solution.py:12
  101.9 7.1 %collective-permute-start.11 = (f32[20,64]{1,0:T(8,128)S(1)}, f32[20,64]{1,0:T(8,128)S(1)}, u32[]{:S(2)}, u32[]{:S(2)}) collective-permute-start(f32[20,64]{1,0:T(8,128)S(1)} %bitcast.123), channel_id=1, source_target_pairs={{16,0},{0,16},{17,1},{1,17},{18,2},{2,18},{19,3},{3,19},{20,4},{4,... | collective-permute-start | bytes 15368 | tf_op jit(solution)/shard_map/ppermute | solution.py:12
  106.8 3.6 %collective-permute-start.9 = (f32[20,128]{1,0:T(8,128)S(1)}, f32[20,128]{1,0:T(8,128)S(1)}, u32[]{:S(2)}, u32[]{:S(2)}) collective-permute-start(f32[20,128]{1,0:T(8,128)S(1)} %slice_bitcast_fusion.8), channel_id=1, source_target_pairs={{1,0},{2,1},{3,2},{4,3},{5,4},{6,5},{7,6},{8,7},{9,8},{10,9},{11,1... | collective-permute-start | bytes 30728 | tf_op jit(solution)/shard_map/ppermute | solution.py:12
  (5 other events, 4.9 us)
